TPU v7x, 256 devices: a whole 4x4x8 slice. The times are simulated.
256 devices in a mesh: row: 16 (over y_hi, z), col: 16 (over y_lo, x, core).
Axes of the slice: x: 4, y: 4 (y_hi: 2, y_lo: 2; y = y_hi * 2 + y_lo), z: 8, core: 2. Of those that a mesh axis runs over, the one named last changes fastest.
Arguments:
- x_tiles: bfloat16 [256, 2048, 128], P('row', 'col'), may hold values from -1.328125 to 1.328125
- tile_pos: int32 [16, 256], P('row', 'col'), may hold values from 0 to 63, as said below
- panel_ids: int32 [4], replicated, may hold values from 0 to 31, as said below
Outputs:
- square_part: float32 [16384, 16384], P('row', 'col')
Inputs may be any that keep to these rules, and one draw needn't show every extreme that they name: `tile_pos`: on each device the 16 positions are distinct and increasing. Split the device's 8 x 8 local blocks into squares of 4 x 4 blocks aligned to multiples of 4: one square (drawn) holds exactly 10 stored blocks and every other square exactly 2. `panel_ids`: the 4 panels are distinct, and one of them is the last panel.
All inputs are finite; a program needn't handle non-finite values.
Results may differ from a plain program's by a relative error of at most 0.0003.
Values may be sent and summed in bfloat16 or wider, within the bound.
A program may use at most 64 MiB of HBM per device.

v0:
```python
import jax
import jax.numpy as jnp
from jax import lax
from jax.sharding import PartitionSpec as P

LR = 8
PW = 4
SECTIONS = 4


def spread(shard, axis, root):
    mine = lax.axis_index(axis) == root
    return lax.psum(jnp.where(mine, shard, jnp.zeros_like(shard)), axis)


def per_device(x_tiles, tile_pos, panel_ids):
    blocksz = x_tiles.shape[1]
    col_count = LR * lax.axis_size("row") // lax.axis_size("col")
    positions = tile_pos[0]
    local_rows = positions // col_count
    local_cols = positions % col_count
    grid = (
        jnp.zeros((LR, col_count, blocksz, blocksz), x_tiles.dtype)
        .at[local_rows, local_cols]
        .set(x_tiles)
    )
    dense = grid.transpose(0, 2, 1, 3).reshape(LR * blocksz, col_count * blocksz)
    result = jnp.zeros((LR * blocksz, col_count * blocksz), jnp.float32)
    for section in range(SECTIONS):
        first = panel_ids[section] * PW
        owner_col = first // col_count
        col_offset = first - owner_col * col_count
        owner_row = first // LR
        row_offset = first - owner_row * LR
        column_piece = lax.dynamic_slice_in_dim(dense, col_offset * blocksz, PW * blocksz, 1)
        column_panel = spread(column_piece, "col", owner_col)
        row_piece = lax.dynamic_slice_in_dim(dense, row_offset * blocksz, PW * blocksz, 0)
        row_panel = spread(row_piece, "row", owner_row)
        result = result + jnp.dot(column_panel, row_panel, preferred_element_type=jnp.float32)
    return result


def solution(mesh):
    in_specs = (P("row", "col", None), P("row", "col"), P())
    out_specs = P("row", "col")
    return jax.shard_map(
        per_device, mesh=mesh, in_specs=in_specs, out_specs=out_specs, check_vma=False
    )
```

profile of v0, /device:TPU:1, one launch (start us, length us, event | category | flops | bytes accessed | tf_op | source)
XLA Modules:
  0.0 348.4 jit_solution(18093487347870322191)
XLA Ops:
  6.5 0.0 all-reduce.7.cloned.1.call-start
  6.5 1.4 fusion.2
  10.6 0.7 fusion.1
  11.2 0.5 broadcast_in_dim.2
  11.8 2.2 scatter_fusion
  14.0 1.4 copy.4
  15.4 0.6 copy.7
  16.0 2.8 dynamic-slice_select_fusion
  18.8 0.0 all-reduce.7.cloned.1.call-update
  18.8 0.0 all-reduce.5.cloned.1.call-start
  18.9 2.9 dynamic-slice_select_fusion.1
  21.7 0.0 all-reduce.5.cloned.1.call-update
  21.8 166.8 %all-reduce.7.cloned.1.call-done = (bf16[512,1024]{1,0:T(8,128)(2,1)}, bf16[512,1024]{1,0:T(8,128)(2,1)}, bf16[512,1024]{1,0:T(8,128)(2,1)}, bf16[512,1024]{1,0:T(8,128)(2,1)}) async-done(((bf16[512,1024]{1,0:T(8,128)(2,1)}, bf16[512,1024]{1,0:T(8,128)(2,1)}, bf16[512,1024]{1,0:T(8,128)(2,1)}, bf16[512,1024]{1,0:T(8,128)(2,1)}), (bf16[512,1024]{1,0:T(8,128)(2,1)}, bf16[512,1024]{1,0:T(8,128)(2,1)}, ...) | async-done | bytes 4194320 | tf_op jit(solution)/shard_map/psum | solution.py:13
  188.6 143.5 %all-reduce.5.cloned.1.call-done = (bf16[1024,512]{1,0:T(8,128)(2,1)}, bf16[1024,512]{1,0:T(8,128)(2,1)}, bf16[1024,512]{1,0:T(8,128)(2,1)}, bf16[1024,512]{1,0:T(8,128)(2,1)}) async-done(((bf16[1024,512]{1,0:T(8,128)(2,1)}, bf16[1024,512]{1,0:T(8,128)(2,1)}, bf16[1024,512]{1,0:T(8,128)(2,1)}, bf16[1024,512]{1,0:T(8,128)(2,1)}), (bf16[1024,512]{1,0:T(8,128)(2,1)}, bf16[1024,512]{1,0:T(8,128)(2,1)}, ...) | async-done | bytes 4194320 | tf_op jit(solution)/shard_map/psum | solution.py:13
  332.2 0.0 copy-start.3
  332.2 0.0 copy-start.5
  332.2 2.9 fusion.5
  335.1 0.0 copy-done.3
  335.1 0.0 copy-done.5
  335.1 0.0 copy-start.2
  335.1 0.0 copy-start.4
  335.1 1.3 fusion.3
  336.4 0.0 copy-done.2
  336.4 0.3 copy-done.4
  336.7 0.0 copy-start
  336.7 0.0 copy-start.1
  336.7 1.2 fusion.4
  337.9 0.0 copy-done
  337.9 0.3 copy-done.1
  338.2 3.3 add_add_fusion
Async XLA Ops:
  6.5 182.1 %all-reduce.7.cloned.1.call-start = ((), (), s32[]{:S(2)}) async-start(), calls=%async_computation.1 | async-start | bytes 8388608 | tf_op jit(solution)/shard_map/psum | solution.py:13
  18.8 313.3 %all-reduce.5.cloned.1.call-start = ((), (), s32[]{:S(2)}) async-start(), calls=%async_computation | async-start | bytes 8388608 | tf_op jit(solution)/shard_map/psum | solution.py:13
  332.2 2.9 copy-start.3
  332.2 3.0 copy-start.5
  335.1 1.3 copy-start.2
  335.1 1.5 copy-start.4
  336.7 1.3 copy-start
  336.7 1.5 copy-start.1
Sparse Core Ops, SparseCore 0:
  18.9 169.6 all-reduce.6
  191.5 140.6 all-reduce.4
where the time goes:
time: 349 us; the launch traced here: 348 us
  waiting for transfers between devices  310 us (89%)
  between operations  16.1 us (5%)
  matrix products  8.76 us (3%)
  local copies, waits for them, and re-layouts  6.73 us (2%)
  other arithmetic  6.29 us (2%)
    psum x2, waiting for transfers between devices, spread(): return lax.psum(jnp.where(mine, shard, jnp.zeros_like(shard)), axis)  310 us
    dot_general x4, matrix products, per_device(): jnp.dot(column_panel, row_panel, preferred_element_type=jnp.float32)  8.76 us
  transfers between devices with their start and end apart: 2, of which 2 were waited for; matrix products, arithmetic and copies ran while one was open for 1% of the time, Pallas kernels for 0%

commit v1 on v0

v1 whole, which is shorter than its diff:
```python
import functools

import jax
import jax.numpy as jnp
from jax import lax
from jax.experimental import pallas as pl
from jax.experimental.pallas import tpu as pltpu
from jax.sharding import PartitionSpec as P

BS = 128
LR = 8
LC = 8
PW = 4
SECTIONS = 4
SLOTS = 16
WIN = 12
HALF_WIN = WIN // 2
LOW = SLOTS - WIN
CH = 32
NZ, NX = 8, 4
MB, MA = 2, 1
NB_R = HALF_WIN * (BS // CH)
NA_R = HALF_WIN * (BS // 2 // CH)
SB_R = NB_R + (NZ - 1) * MB
TB_R = SB_R - MB
SA_R = NA_R + (NX - 1) * MA
TA_R = SA_R - MA
MESH = pl.DeviceIdType.MESH

NEEDED = []
for _i in range(HALF_WIN):
    _all = [_i, _i + LOW, _i + HALF_WIN, _i + HALF_WIN + LOW]
    NEEDED.append([s for s in _all if all(s not in prev for prev in NEEDED)])


def sort_kernel(pos, x_ref, o_ref):
    def count(s, n):
        return n + jnp.where((pos[0, s] % LC) < PW, 1, 0)

    left = lax.fori_loop(0, SLOTS, count, 0)

    def place(s, carry):
        a, b = carry
        is_left = (pos[0, s] % LC) < PW
        o_ref[jnp.where(is_left, a, b)] = x_ref[s]
        one = jnp.where(is_left, 1, 0)
        return a + one, b + 1 - one

    lax.fori_loop(0, SLOTS, place, (0, left))


def comm_kernel(
    panels, x_ref, xa_ref, sb, sa, sx,
    pb, pa, rb, ra,
    xb_send, xa_send, xb_recv, xa_recv,
    b_send, b_recv, a_send, a_recv, s_send, s_recv,
):
    row = lax.axis_index("row")
    col = lax.axis_index("col")
    core = lax.rem(col, 2)
    z, yh = lax.rem(row, NZ), row // NZ
    x, yl = lax.rem(col // 2, NX), col // 8

    def rowdev(zz, yy):
        return {"row": yy * NZ + zz, "col": col}

    def coldev(xx, yy, cc):
        return {"row": row, "col": (yy * NX + xx) * 2 + cc}

    z_to = [rowdev(lax.rem(z + 1, NZ), yh), rowdev(lax.rem(z + NZ - 1, NZ), yh)]
    x_to = [coldev(lax.rem(x + 1, NX), yl, core), coldev(lax.rem(x + NX - 1, NX), yl, core)]
    y_row = rowdev(z, 1 - yh)
    sibling = coldev(x, yl, 1 - core)
    y_col = coldev(x, 1 - yl, core)
    diag = coldev(x, 1 - yl, 1 - core)

    barrier = pltpu.get_barrier_semaphore()
    peers = z_to + x_to + [y_row, sibling, y_col, diag]
    for dev in peers:
        pl.semaphore_signal(barrier, inc=1, device_id=dev, device_id_type=MESH)
    pl.semaphore_wait(barrier, len(peers))

    mine = pl.ds(pl.multiple_of(core * 64, 64), 64)
    other = pl.ds(pl.multiple_of((1 - core) * 64, 64), 64)

    def b_hand(s):
        return pltpu.make_async_remote_copy(
            src_ref=x_ref.at[s], dst_ref=pb.at[s], send_sem=xb_send, recv_sem=xb_recv.at[s],
            device_id=y_row, device_id_type=MESH)

    def a_hand(j, s):
        dev, rows = [(sibling, other), (y_col, mine), (diag, other)][j]
        return pltpu.make_async_remote_copy(
            src_ref=xa_ref.at[s, rows], dst_ref=pa.at[j, s], send_sem=xa_send.at[j],
            recv_sem=xa_recv.at[j, s], device_id=dev, device_id_type=MESH)

    for slots in NEEDED:
        for s in slots:
            b_hand(s).start()
            for j in range(3):
                a_hand(j, s).start()

    def b_copy(d, t):
        return pltpu.make_async_remote_copy(
            src_ref=sb.at[d, t], dst_ref=rb.at[d, t], send_sem=b_send.at[d],
            recv_sem=b_recv.at[d, t], device_id=z_to[d], device_id_type=MESH)

    def a_copy(d, t):
        return pltpu.make_async_remote_copy(
            src_ref=sa.at[d, t], dst_ref=ra.at[d, t], send_sem=a_send.at[d],
            recv_sem=a_recv.at[d, t], device_id=x_to[d], device_id_type=MESH)

    def s_copy(d, t):
        return pltpu.make_async_remote_copy(
            src_ref=sa.at[d, t], dst_ref=sx.at[d, t], send_sem=s_send.at[d],
            recv_sem=s_recv.at[d], device_id=sibling, device_id_type=MESH)

    owner = [panels[k] // 2 for k in range(SECTIONS)]
    high = [panels[k] % 2 == 1 for k in range(SECTIONS)]
    b_own = [owner[k] == row for k in range(SECTIONS)]
    b_oth = [owner[k] == (1 - yh) * NZ + z for k in range(SECTIONS)]

    def at(cc, yy):
        return [owner[k] == (yy * NX + x) * 2 + cc for k in range(SECTIONS)]

    a_own = at(core, yl)
    a_oth = [at(1 - core, yl), at(core, 1 - yl), at(1 - core, 1 - yl)]

    def b_round(t, i, q, first):
        rows = pl.ds(q * CH, CH)
        for d in range(2):
            s0 = i + HALF_WIN * d
            if not first:
                b_copy(d, t - MB).wait_recv()
            own = x_ref[s0, rows, :], x_ref[s0 + LOW, rows, :]
            oth = pb[s0, rows, :], pb[s0 + LOW, rows, :]
            for k in range(SECTIONS):
                v = lax.select(high[k], oth[1], oth[0])
                if not first:
                    v = lax.select(b_oth[k], v, rb[d, t - MB, k])
                v = lax.select(b_own[k], lax.select(high[k], own[1], own[0]), v)
                sb[d, t, k] = v
            b_copy(d, t).start()

    def a_round(t, i, q, first):
        rows = pl.ds(q * CH, CH)
        own_rows = pl.ds(pl.multiple_of(core * 64 + q * CH, CH), CH)
        for d in range(2):
            s0 = i + HALF_WIN * d
            if not first:
                a_copy(d, t - MA).wait_recv()
            own = xa_ref[s0, own_rows, :], xa_ref[s0 + LOW, own_rows, :]
            oth = [(pa[j, s0, rows, :], pa[j, s0 + LOW, rows, :]) for j in range(3)]
            for k in range(SECTIONS):
                v = own[0] if first else ra[d, t - MA, k]
                v = lax.select(a_own[k], lax.select(high[k], own[1], own[0]), v)
                for j in range(3):
                    v = lax.select(a_oth[j][k], lax.select(high[k], oth[j][1], oth[j][0]), v)
                sa[d, t, k] = v
            a_copy(d, t).start()
            s_copy(d, t).start()

    for i in range(HALF_WIN):
        for s in NEEDED[i]:
            b_hand(s).wait_recv()
            for j in range(3):
                a_hand(j, s).wait_recv()

        def pair(h, _, i=i):
            a_round(2 * i + h, i, h, False)
            b_round(4 * i + 2 * h, i, 2 * h, False)
            b_round(4 * i + 2 * h + 1, i, 2 * h + 1, False)
            return 0

        if i == 0:
            for t in range(4):
                if t % 2 == 0:
                    a_round(t // 2, 0, t // 2, t // 2 < MA)
                b_round(t, 0, t, t < MB)
        else:
            lax.fori_loop(0, 2, pair, 0)

    def a_tail(t, _):
        for d in range(2):
            a_copy(d, t - MA).wait_recv()
            sa[d, t] = ra[d, t - MA]
            @pl.when(t < TA_R)
            def _():
                a_copy(d, t).start()
            s_copy(d, t).start()
        return 0

    def b_tail(t, _):
        for d in range(2):
            b_copy(d, t - MB).wait_recv()
            sb[d, t] = rb[d, t - MB]
            @pl.when(t < TB_R)
            def _():
                b_copy(d, t).start()
        return 0

    def both_tail(j, _):
        a_tail(NA_R + j, 0)
        for u in range(2):
            b_tail(NB_R + 2 * j + u, 0)
        return 0

    joint = SA_R - NA_R
    lax.fori_loop(0, joint, both_tail, 0)
    lax.fori_loop(NB_R + 2 * joint, SB_R, b_tail, 0)

    pltpu.make_async_copy(x_ref, x_ref, xb_send).wait()
    for j in range(3):
        pltpu.make_async_copy(pa.at[j], pa.at[j], xa_send.at[j]).wait()
    for d in range(2):
        sent = sb.at[d, pl.ds(0, TB_R)]
        pltpu.make_async_copy(sent, sent, b_send.at[d]).wait()
        sent = sa.at[d, pl.ds(0, TA_R)]
        pltpu.make_async_copy(sent, sent, a_send.at[d]).wait()
        pltpu.make_async_copy(sa.at[d], sa.at[d], s_send.at[d]).wait()
        pltpu.make_async_copy(sx.at[d], sx.at[d], s_recv.at[d]).wait()


def product_kernel(panels, pos_a, pos_b, where_am_i, sb, sa, sx, c_ref, a_full, b_full):
    @pl.when(pl.program_id(0) == 0)
    def _():
        row, col = where_am_i[0], where_am_i[1]
        z, x, core = row % NZ, (col // 2) % NX, col % 2
        a_full[...] = jnp.zeros_like(a_full)
        b_full[...] = jnp.zeros_like(b_full)

        def section(k, _):
            panel = panels[k]
            owner = panel // 2
            high = panel % 2
            zo, xo = owner % NZ, (owner // 2) % NX
            db = [(z - zo + NZ) % NZ, (zo - z + NZ) % NZ]
            da = [(x - xo + NX) % NX, (xo - x + NX) % NX]

            def left(s, n):
                return n + jnp.where((pos_a[owner, s] % LC) < PW, 1, 0)

            skip = jnp.where(high == 1, lax.fori_loop(0, SLOTS, left, 0) - LOW, 0)

            def tile(s, w):
                p = pos_b[owner, s]
                @pl.when((p // LC) // PW == high)
                def _():
                    wb = s - LOW * high
                    d = wb // HALF_WIN
                    t = jnp.where(d == 0, db[0], db[1]) * MB + (wb % HALF_WIN) * (BS // CH)
                    kk = (p // LC) % PW
                    r0 = pl.multiple_of((k * PW + kk) * BS, BS)
                    c0 = pl.multiple_of((p % LC) * BS, BS)
                    v = sb[d, pl.ds(t, BS // CH), k].reshape(BS, BS)
                    b_full[pl.ds(r0, BS), pl.ds(c0, BS)] = v
                p = pos_a[owner, s]
                hit = (p % LC) // PW == high
                @pl.when(hit)
                def _():
                    d = w // HALF_WIN
                    t = jnp.where(d == 0, da[0], da[1]) * MA + (w % HALF_WIN) * (BS // 2 // CH)
                    kk = (p % LC) % PW
                    r0 = pl.multiple_of((p // LC) * BS, BS)
                    c0 = pl.multiple_of((k * PW + kk) * BS, BS)
                    ours = sa[d, pl.ds(t, BS // 2 // CH), k].reshape(BS // 2, BS)
                    theirs = sx[d, pl.ds(t, BS // 2 // CH), k].reshape(BS // 2, BS)
                    r1 = pl.multiple_of(r0 + core * 64, 64)
                    r2 = pl.multiple_of(r0 + (1 - core) * 64, 64)
                    a_full[pl.ds(r1, BS // 2), pl.ds(c0, BS)] = ours
                    a_full[pl.ds(r2, BS // 2), pl.ds(c0, BS)] = theirs
                return w + jnp.where(hit, 1, 0)

            lax.fori_loop(0, SLOTS, tile, skip)
            return 0

        lax.fori_loop(0, SECTIONS, section, 0)

    rows = c_ref.shape[0]
    r0 = pl.multiple_of(pl.program_id(0) * rows, rows)
    c_ref[...] = jnp.dot(
        a_full[pl.ds(r0, rows), :], b_full[...], preferred_element_type=jnp.float32)


def per_device(x_tiles, tile_pos, panel_ids):
    vmem = pl.BlockSpec(memory_space=pltpu.VMEM)
    smem = pl.BlockSpec(memory_space=pltpu.SMEM)
    bf16 = jnp.bfloat16
    pos_a = lax.all_gather(tile_pos[0], "col")
    pos_b = lax.all_gather(tile_pos[0], "row")
    xa = pl.pallas_call(
        sort_kernel,
        out_shape=jax.ShapeDtypeStruct((SLOTS, BS, BS), bf16),
        in_specs=[smem, vmem],
        out_specs=vmem,
        name="sort_slots",
    )(tile_pos, x_tiles)
    dma = pltpu.SemaphoreType.DMA
    sb, sa, sx = pl.pallas_call(
        comm_kernel,
        out_shape=[
            jax.ShapeDtypeStruct((2, SB_R, SECTIONS, CH, BS), bf16),
            jax.ShapeDtypeStruct((2, SA_R, SECTIONS, CH, BS), bf16),
            jax.ShapeDtypeStruct((2, SA_R, SECTIONS, CH, BS), bf16),
        ],
        in_specs=[smem, vmem, vmem],
        out_specs=[vmem, vmem, vmem],
        scratch_shapes=[
            pltpu.VMEM((SLOTS, BS, BS), bf16),
            pltpu.VMEM((3, SLOTS, BS // 2, BS), bf16),
            pltpu.VMEM((2, TB_R, SECTIONS, CH, BS), bf16),
            pltpu.VMEM((2, TA_R, SECTIONS, CH, BS), bf16),
            dma, dma((3,)), dma((SLOTS,)), dma((3, SLOTS)),
            dma((2,)), dma((2, TB_R)), dma((2,)), dma((2, TA_R)), dma((2,)), dma((2,)),
        ],
        compiler_params=pltpu.CompilerParams(
            collective_id=0, has_side_effects=True, vmem_limit_bytes=40 << 20),
        name="spread_tiles",
    )(panel_ids, x_tiles, xa)
    here = jnp.stack([lax.axis_index("row"), lax.axis_index("col")]).astype(jnp.int32)
    n = LR * BS
    kdim = SECTIONS * PW * BS
    steps = 4
    return pl.pallas_call(
        product_kernel,
        out_shape=jax.ShapeDtypeStruct((n, LC * BS), jnp.float32),
        grid=(steps,),
        in_specs=[smem, smem, smem, smem, vmem, vmem, vmem],
        out_specs=pl.BlockSpec((n // steps, LC * BS), lambda i: (i, 0)),
        scratch_shapes=[pltpu.VMEM((n, kdim), bf16), pltpu.VMEM((kdim, LC * BS), bf16)],
        compiler_params=pltpu.CompilerParams(vmem_limit_bytes=48 << 20),
        cost_estimate=pl.CostEstimate(
            flops=2 * n * kdim * LC * BS, bytes_accessed=10 << 20, transcendentals=0),
        name="panel_product",
    )(panel_ids, pos_a, pos_b, here, sb, sa, sx)


def solution(mesh):
    in_specs = (P("row", "col", None), P("row", "col"), P())
    out_specs = P("row", "col")
    return jax.shard_map(
        per_device, mesh=mesh, in_specs=in_specs, out_specs=out_specs, check_vma=False
    )
```

time: 349 us -> 153 us (0.44)
  the two profiles are of different devices: /device:TPU:1 before, /device:TPU:2 now
where the time goes in v1:
time: 153 us; the launch traced here: 152 us
  Pallas kernels  88.5 us (58%)
  blocking collectives  60.4 us (39%)
  local copies, waits for them, and re-layouts  3.39 us (2%)
    pallas_call x1, Pallas kernels, per_device(): pl.pallas_call(comm_kernel, out_shape=[jax.ShapeDtypeStruct((2, SB_R, SEC...  72.9 us
    all_gather x1, blocking collectives, per_device(): pos_b = lax.all_gather(tile_pos[0], 'row')  44 us
    all_gather x1, blocking collectives, per_device(): pos_a = lax.all_gather(tile_pos[0], 'col')  16.5 us
    pallas_call x1, Pallas kernels, per_device(): pl.pallas_call(product_kernel, out_shape=jax.ShapeDtypeStruct((n, LC * BS...  13.3 us
    unnamed x8, local copies, waits for them, and re-layouts  3.39 us

profile of v1, /device:TPU:2, one launch (start us, length us, event | category | flops | bytes accessed | tf_op | source)
XLA Modules:
  0.0 152.4 jit_solution(7056634702702586987)
XLA Ops:
  0.0 0.1 pad_add_fusion.where_am_i
  0.1 44.0 %all-gather.1 = s32[16,1,16]{2,1,0:T(1,128)S(1)} all-gather(s32[1,1,16]{2,1,0:T(1,128)} %bitcast.7), channel_id=1, replica_groups=mesh['row'=16,'col'=16] {'row'}, dimensions={0}, use_global_device_ids=true | all-gather | bytes 1088 | tf_op jit(solution)/shard_map/all_gather | solution.py:290
  44.0 16.5 %all-gather = s32[16,1,16]{2,1,0:T(1,128)S(1)} all-gather(s32[1,1,16]{2,1,0:T(1,128)} %bitcast.8), channel_id=1, replica_groups=mesh['row'=16,'col'=16] {'col'}, dimensions={0}, use_global_device_ids=true | all-gather | bytes 1088 | tf_op jit(solution)/shard_map/all_gather | solution.py:289
  60.5 2.2 %sort_slots.1.xa_ref = bf16[16,128,128]{2,1,0:T(8,128)(2,1)} custom-call(s32[1,16]{1,0:T(1,128)} %pos.1, bf16[16,128,128]{2,1,0:T(8,128)(2,1)} %x_ref.3), custom_call_target="tpu_custom_call" | custom-call | tf_op jit(solution)/shard_map/sort_slots/pallas_call | solution.py:291
  62.7 0.0 copy-start
  62.7 1.0 copy-done
  63.8 0.0 copy-start.1
  63.8 1.0 copy-done.1
  64.8 0.0 copy-start.2
  64.8 0.7 copy-done.2
  65.5 72.9 %spread_tiles.1 = (bf16[2,38,4,32,128]{4,3,2,1,0:T(8,128)(2,1)S(1)}, bf16[2,15,4,32,128]{4,3,2,1,0:T(8,128)(2,1)S(1)}, bf16[2,15,4,32,128]{4,3,2,1,0:T(8,128)(2,1)S(1)}) custom-call(s32[4]{0:T(128)S(1)} %copy-done.2, bf16[16,128,128]{2,1,0:T(8,128)(2,1)S(1)} %copy-done, bf16[16,128,128]{2,1,0:T(8,128)(2,1)S(1)} %copy-done.1), custom_call_target="tpu_custom_call" | custom-call | tf_op jit(solution)/shard_map/spread_tiles/pallas_call | solution.py:299
  138.4 0.0 copy-start.3
  138.4 0.6 copy-done.3
  139.1 13.3 %panel_product.1 = f32[1024,1024]{1,0:T(8,128)} custom-call(s32[4]{0:T(128)S(1)} %copy-done.3, s32[16,16]{1,0:T(8,128)S(1)} %bitcast.6, s32[16,16]{1,0:T(8,128)S(1)} %bitcast.5, s32[2]{0:T(128)S(1)} %pad_add_fusion.where_am_i, bf16[2,38,4,32,128]{4,3,2,1,0:T(8,128)(2,1)S(1)} %get-tuple-element.8.sb, bf16[2,15,4,32,128]{4,3,2,1,0:T(8,128)(2,1)S(1)} %get-tuple-element.9.sa, ...), custom_call_target="tpu_custom_call" | custom-call | flops 4294967296 | bytes 10485760 | tf_op jit(solution)/shard_map/panel_product/pallas_call | solution.py:324
Async XLA Ops:
  62.7 1.0 copy-start
  63.8 1.0 copy-start.1
  64.8 0.7 copy-start.2
  138.4 0.7 copy-start.3

commit v2 on v0

v2 whole, which is shorter than its diff:
```python
import jax
import jax.numpy as jnp
from jax import lax
from jax.experimental import pallas as pl
from jax.experimental.pallas import tpu as pltpu
from jax.sharding import PartitionSpec as P

BS = 128
LR = 8
LC = 8
PW = 4
SECTIONS = 4
SLOTS = 16
WIN = 12
HALF = WIN // 2
LOW = SLOTS - WIN
NZ, NX = 8, 4
CB, CA = 32, 64
MB, MA = 4, 4
QB, QA = BS // CB, BS // CA
NB_R, NA_R = HALF * QB, HALF * QA
TB_R, TA_R = NB_R + (NZ - 2) * MB, NA_R + (NX - 2) * MA
SB_R, SA_R = TB_R + MB, TA_R + MA
MESH = pl.DeviceIdType.MESH

NEEDED = []
for _i in range(HALF):
    _all = [_i, _i + LOW, _i + HALF, _i + HALF + LOW]
    NEEDED.append([s for s in _all if all(s not in prev for prev in NEEDED)])


def comm_kernel(
    panels, pos, x_hbm, sb, sa, meta,
    xv, xa, pc, rb, ra, mo, mc, mb, ma, mt,
    x_sem, h_send, h_recv, b_send, b_recv, a_send, a_recv, s_send, s_recv,
    mh_send, mh_recv, mr_send, mr_recv, mf_send, mf_recv,
):
    row = lax.axis_index("row")
    col = lax.axis_index("col")
    core = lax.rem(col, 2)
    z, yh = lax.rem(row, NZ), row // NZ
    x, yl = lax.rem(col // 2, NX), col // 8

    def dev(zz, yyh, xx, yyl, cc):
        return {"row": yyh * NZ + zz, "col": (yyl * NX + xx) * 2 + cc}

    z_to = [dev(lax.rem(z + 1, NZ), yh, x, yl, core), dev(lax.rem(z + NZ - 1, NZ), yh, x, yl, core)]
    x_to = [dev(z, yh, lax.rem(x + 1, NX), yl, core), dev(z, yh, lax.rem(x + NX - 1, NX), yl, core)]
    sibling = dev(z, yh, x, yl, 1 - core)
    yh_same, yh_cross = dev(z, 1 - yh, x, yl, core), dev(z, 1 - yh, x, yl, 1 - core)
    yl_same, yl_cross = dev(z, yh, x, 1 - yl, core), dev(z, yh, x, 1 - yl, 1 - core)

    def remote(src, dst, send, recv, to):
        return pltpu.make_async_remote_copy(
            src_ref=src, dst_ref=dst, send_sem=send, recv_sem=recv,
            device_id=to, device_id_type=MESH)

    local = pltpu.make_async_copy(x_hbm, xv, x_sem)
    local.start()
    barrier = pltpu.get_barrier_semaphore()

    def greet(peers):
        for peer in peers:
            pl.semaphore_signal(barrier, inc=1, device_id=peer, device_id_type=MESH)
        pl.semaphore_wait(barrier, len(peers))

    lane = lax.broadcasted_iota(jnp.int32, (8, BS), 1)
    where = jnp.zeros((8, BS), jnp.int32)
    spot = [pos[0, s] for s in range(SLOTS)]
    for s in range(SLOTS):
        where = jnp.where(lane == s, spot[s], where)
    mo[...] = where
    right = [lax.rem(p, LC) // PW for p in spot]
    n_left = SLOTS - sum(right)
    lefts, rights, rank = 0, n_left, []
    for s in range(SLOTS):
        rank.append(jnp.where(right[s] == 0, lefts, rights))
        lefts, rights = lefts + 1 - right[s], rights + right[s]
    local.wait()
    for i in range(SLOTS):
        src = sum(jnp.where(rank[s] == i, s, 0) for s in range(SLOTS))
        xa[i] = xv[src]

    owner = [panels[k] // 2 for k in range(SECTIONS)]
    high = [lax.rem(panels[k], 2) == 1 for k in range(SECTIONS)]

    def hand(source, to, j, s):
        return remote(source.at[s], pc.at[j, s], h_send.at[j], h_recv.at[j, s], to)

    def hand_meta(to, j):
        return remote(mo, mc.at[j], mh_send.at[j], mh_recv.at[j], to)

    def hand_over(plan):
        for _, to, j in plan:
            hand_meta(to, j).start()
        for slots in NEEDED:
            for s in slots:
                for source, to, j in plan:
                    hand(source, to, j, s).start()

    def handed(i):
        for s in NEEDED[i]:
            for j in range(3):
                hand(xv, sibling, j, s).wait_recv()

    def handed_meta():
        for j in range(3):
            hand_meta(sibling, j).wait_recv()

    def all_left(ref, sem):
        pltpu.make_async_copy(ref, ref, sem).wait()

    def pick(own, low_high, cond, v):
        return lax.select(cond, lax.select(own, low_high[1], low_high[0]), v)

    def b_copy(d, t):
        return remote(sb.at[d, t], rb.at[d, t], b_send.at[d], b_recv.at[d, t], z_to[d])

    def b_share(d, t):
        return remote(sb.at[d, t, 0], sb.at[d, t, 0], s_send.at[d], s_recv.at[d], sibling)

    def b_meta(j):
        return remote(mb.at[j], mb.at[j + 1], mr_send, mr_recv.at[j], z_to[0])

    @pl.when(core == 1)
    def _():
        greet(z_to + [sibling, yh_same, yh_cross, yl_cross])
        hand_over([(xa, sibling, 0), (xv, yh_same, 1), (xa, yl_cross, 2)])
        own_here = [owner[k] == row for k in range(SECTIONS)]
        own_there = [owner[k] == (1 - yh) * NZ + z for k in range(SECTIONS)]

        def b_round(t, i, q, first):
            rows = pl.ds(q * CB, CB)
            for d in range(2):
                s0 = i + HALF * d
                if not first:
                    b_copy(d, t - MB).wait_recv()
                for cc in range(2):
                    if cc == 1:
                        here = xv[s0, rows, :], xv[s0 + LOW, rows, :]
                    else:
                        here = pc[0, s0, rows, :], pc[0, s0 + LOW, rows, :]
                    j = 2 - cc
                    there = pc[j, s0, rows, :], pc[j, s0 + LOW, rows, :]
                    for k in range(SECTIONS):
                        v = here[0] if first else rb[d, t - MB, cc, k]
                        v = pick(high[k], there, own_there[k], v)
                        v = pick(high[k], here, own_here[k], v)
                        sb[d, t, cc, k] = v
                b_copy(d, t).start()
                b_share(d, t).start()

        for i in range(HALF):
            handed(i)
            if i == 0:
                handed_meta()
                for cc in range(2):
                    here = mo[0:1, :] if cc == 1 else mc[0, 0:1, :]
                    there = mc[2 - cc, 0:1, :]
                    for k in range(SECTIONS):
                        r = cc * SECTIONS + k
                        mb[0, r : r + 1, :] = jnp.where(own_here[k], here, there)
            else:
                b_meta(i - 1).wait_recv()
            b_meta(i).start()
            if i * QB < MB:
                for q in range(QB):
                    b_round(i * QB + q, i, q, i * QB + q < MB)
            else:
                def step(q, _, i=i):
                    b_round(i * QB + q, i, q, False)
                    return 0

                lax.fori_loop(0, QB, step, 0)

        b_meta(HALF - 1).wait_recv()
        b_meta(HALF).start()

        def tail(t, _):
            for d in range(2):
                b_copy(d, t - MB).wait_recv()
                sb[d, t] = rb[d, t - MB]

                @pl.when(t < TB_R)
                def _():
                    b_copy(d, t).start()

                b_share(d, t).start()
            return 0

        lax.fori_loop(NB_R, SB_R, tail, 0)
        b_meta(HALF).wait_recv()
        for k in range(SECTIONS):
            far = lax.rem(z - lax.rem(owner[k], NZ) + NZ, NZ)
            hops = mb[far]
            meta[0, k : k + 1, :] = hops[SECTIONS + k : SECTIONS + k + 1, :]
            mt[k : k + 1, :] = hops[k : k + 1, :]
        final = remote(mt, meta.at[0], mf_send, mf_recv, sibling)
        final.start()
        for d in range(2):
            all_left(sb.at[d, pl.ds(0, TB_R)], b_send.at[d])
            all_left(sb.at[d, pl.ds(0, SB_R), 0], s_send.at[d])
            all_left(sa.at[d], s_recv.at[d])
        all_left(mb.at[pl.ds(0, NZ - 1)], mr_send)
        all_left(mt, mf_send)
        all_left(mt, mf_recv)

    def a_copy(d, t):
        return remote(sa.at[d, t], ra.at[d, t], a_send.at[d], a_recv.at[d, t], x_to[d])

    def a_share(d, t):
        return remote(sa.at[d, t], sa.at[d, t], s_send.at[d], s_recv.at[d], sibling)

    def a_meta(j):
        return remote(ma.at[j], ma.at[j + 1], mr_send, mr_recv.at[j], x_to[0])

    @pl.when(core == 0)
    def _():
        greet(x_to + [sibling, yl_same, yl_cross, yh_cross])
        hand_over([(xv, sibling, 0), (xa, yl_same, 1), (xv, yh_cross, 2)])

        def at(cc, yy):
            return [owner[k] == (yy * NX + x) * 2 + cc for k in range(SECTIONS)]

        own = [at(0, yl), at(1, yl), at(0, 1 - yl), at(1, 1 - yl)]

        def a_round(t, i, q, first):
            rows = pl.ds(q * CA, CA)
            for d in range(2):
                s0 = i + HALF * d
                if not first:
                    a_copy(d, t - MA).wait_recv()
                had = [(xa[s0, rows, :], xa[s0 + LOW, rows, :])]
                for j in range(3):
                    had.append((pc[j, s0, rows, :], pc[j, s0 + LOW, rows, :]))
                for k in range(SECTIONS):
                    v = had[0][0] if first else ra[d, t - MA, k]
                    for j in range(4):
                        v = pick(high[k], had[j], own[j][k], v)
                    sa[d, t, k] = v
                a_copy(d, t).start()
                a_share(d, t).start()

        for i in range(HALF):
            handed(i)
            if i == 0:
                handed_meta()
                for k in range(SECTIONS):
                    v = mo[0:1, :]
                    for j in range(3):
                        v = jnp.where(own[j + 1][k], mc[j, 0:1, :], v)
                    ma[0, k : k + 1, :] = v
                    ma[0, SECTIONS + k : SECTIONS + k + 1, :] = v
                a_meta(0).start()
            elif i < NX - 1:
                a_meta(i - 1).wait_recv()
                a_meta(i).start()
            if i * QA < MA:
                for q in range(QA):
                    a_round(i * QA + q, i, q, i * QA + q < MA)
            else:
                def step(q, _, i=i):
                    a_round(i * QA + q, i, q, False)
                    return 0

                lax.fori_loop(0, QA, step, 0)

        def tail(t, _):
            for d in range(2):
                a_copy(d, t - MA).wait_recv()
                sa[d, t] = ra[d, t - MA]

                @pl.when(t < TA_R)
                def _():
                    a_copy(d, t).start()

                a_share(d, t).start()
            return 0

        lax.fori_loop(NA_R, SA_R, tail, 0)
        a_meta(NX - 2).wait_recv()
        for k in range(SECTIONS):
            far = lax.rem(x - lax.rem(owner[k] // 2, NX) + NX, NX)
            meta[1, k : k + 1, :] = ma[far][k : k + 1, :]
            mt[k : k + 1, :] = ma[far][k : k + 1, :]
        final = remote(mt, meta.at[1], mf_send, mf_recv, sibling)
        final.start()
        for d in range(2):
            all_left(sa.at[d, pl.ds(0, TA_R)], a_send.at[d])
            all_left(sa.at[d], s_send.at[d])
            all_left(sb.at[d, pl.ds(0, SB_R), 0], s_recv.at[d])
        all_left(ma.at[pl.ds(0, NX - 1)], mr_send)
        all_left(mt, mf_send)
        all_left(mt, mf_recv)

    for j in range(3):
        all_left(pc.at[j], h_send.at[j])
        all_left(mo, mh_send.at[j])


def product_kernel(panels, here, meta, sb, sa, c_ref, a_full, b_full):
    @pl.when(pl.program_id(0) == 0)
    def _():
        row, col = here[0], here[1]
        z, x, core = row % NZ, (col // 2) % NX, col % 2
        a_full[...] = jnp.zeros_like(a_full)
        b_full[...] = jnp.zeros_like(b_full)

        def section(k, _):
            panel = panels[k]
            owner = panel // 2
            high = panel % 2
            zo, xo = owner % NZ, (owner // 2) % NX
            db = [((z - zo + NZ) % NZ) * MB, ((zo - z + NZ) % NZ) * MB]
            da = [((x - xo + NX) % NX) * MA, ((xo - x + NX) % NX) * MA]

            def left(s, n):
                return n + jnp.where((meta[1, k, s] % LC) < PW, 1, 0)

            skip = jnp.where(high == 1, lax.fori_loop(0, SLOTS, left, 0) - LOW, 0)

            def tile(s, w):
                p = meta[0, k, s]

                @pl.when((p // LC) // PW == high)
                def _():
                    wb = s - LOW * high
                    d = wb // HALF
                    t = jnp.where(d == 0, db[0], db[1]) + (wb % HALF) * QB
                    r0 = pl.multiple_of((k * PW + (p // LC) % PW) * BS, BS)
                    c0 = pl.multiple_of((p % LC) * BS, BS)
                    v = sb[d, pl.ds(t, QB), core, k].reshape(BS, BS)
                    b_full[pl.ds(r0, BS), pl.ds(c0, BS)] = v

                p = meta[1, k, s]
                hit = (p % LC) // PW == high

                @pl.when(hit)
                def _():
                    d = w // HALF
                    t = jnp.where(d == 0, da[0], da[1]) + (w % HALF) * QA
                    r0 = pl.multiple_of((p // LC) * BS, BS)
                    c0 = pl.multiple_of((k * PW + (p % LC) % PW) * BS, BS)
                    v = sa[d, pl.ds(t, QA), k].reshape(BS, BS)
                    a_full[pl.ds(r0, BS), pl.ds(c0, BS)] = v

                return w + jnp.where(hit, 1, 0)

            lax.fori_loop(0, SLOTS, tile, skip)
            return 0

        lax.fori_loop(0, SECTIONS, section, 0)

    rows = c_ref.shape[0]
    r0 = pl.multiple_of(pl.program_id(0) * rows, rows)
    c_ref[...] = jnp.dot(
        a_full[pl.ds(r0, rows), :], b_full[...], preferred_element_type=jnp.float32)


def per_device(x_tiles, tile_pos, panel_ids):
    vmem = pl.BlockSpec(memory_space=pltpu.VMEM)
    smem = pl.BlockSpec(memory_space=pltpu.SMEM)
    bf16, i32 = jnp.bfloat16, jnp.int32
    dma = pltpu.SemaphoreType.DMA
    sb, sa, meta = pl.pallas_call(
        comm_kernel,
        out_shape=[
            jax.ShapeDtypeStruct((2, SB_R, 2, SECTIONS, CB, BS), bf16),
            jax.ShapeDtypeStruct((2, SA_R, SECTIONS, CA, BS), bf16),
            jax.ShapeDtypeStruct((2, 8, BS), i32),
        ],
        in_specs=[smem, smem, pl.BlockSpec(memory_space=pl.ANY)],
        out_specs=[vmem, vmem, vmem],
        scratch_shapes=[
            pltpu.VMEM((SLOTS, BS, BS), bf16),
            pltpu.VMEM((SLOTS, BS, BS), bf16),
            pltpu.VMEM((3, SLOTS, BS, BS), bf16),
            pltpu.VMEM((2, TB_R, 2, SECTIONS, CB, BS), bf16),
            pltpu.VMEM((2, TA_R, SECTIONS, CA, BS), bf16),
            pltpu.VMEM((8, BS), i32),
            pltpu.VMEM((3, 8, BS), i32),
            pltpu.VMEM((NZ, 8, BS), i32),
            pltpu.VMEM((NX, 8, BS), i32),
            pltpu.VMEM((8, BS), i32),
            dma, dma((3,)), dma((3, SLOTS)),
            dma((2,)), dma((2, TB_R)), dma((2,)), dma((2, TA_R)), dma((2,)), dma((2,)),
            dma((3,)), dma((3,)), dma, dma((NZ - 1,)), dma, dma,
        ],
        compiler_params=pltpu.CompilerParams(
            collective_id=0, has_side_effects=True, vmem_limit_bytes=40 << 20),
        name="spread_tiles",
    )(panel_ids, tile_pos, x_tiles)
    here = jnp.stack([lax.axis_index("row"), lax.axis_index("col")]).astype(i32)
    n = LR * BS
    kdim = SECTIONS * PW * BS
    steps = 4
    return pl.pallas_call(
        product_kernel,
        out_shape=jax.ShapeDtypeStruct((n, LC * BS), jnp.float32),
        grid=(steps,),
        in_specs=[smem, smem, smem, vmem, vmem],
        out_specs=pl.BlockSpec((n // steps, LC * BS), lambda i: (i, 0)),
        scratch_shapes=[pltpu.VMEM((n, kdim), bf16), pltpu.VMEM((kdim, LC * BS), bf16)],
        compiler_params=pltpu.CompilerParams(vmem_limit_bytes=48 << 20),
        cost_estimate=pl.CostEstimate(
            flops=2 * n * kdim * LC * BS, bytes_accessed=10 << 20, transcendentals=0),
        name="panel_product",
    )(panel_ids, here, meta, sb, sa)


def solution(mesh):
    in_specs = (P("row", "col", None), P("row", "col"), P())
    out_specs = P("row", "col")
    return jax.shard_map(
        per_device, mesh=mesh, in_specs=in_specs, out_specs=out_specs, check_vma=False
    )
```

time: 349 us -> 84.4 us (0.24)
  waiting for transfers between devices: 310 us -> 0 us
  Pallas kernels: 0 us -> 78.3 us
  between operations: 16.1 us -> 0.02 us
  matrix products: 8.76 us -> 0 us
  other arithmetic: 6.29 us -> 0.07 us
    psum x2 -> x0, waiting for transfers between devices: 310 us -> none  [spread(): return lax.psum(jnp.where(mine, shard, jnp.zeros_like(shard)), axis)]
    pallas_call x0 -> x2, Pallas kernels: none -> 78.3 us  [the longest x1 63.9 us: per_device(): pl.pallas_call(comm_kernel, out_shape=[jax.ShapeDtypeStruct((2, SB_R, 2,...]
    dot_general x4 -> x0, matrix products: 8.76 us -> none  [per_device(): jnp.dot(column_panel, row_panel, preferred_element_type=jnp.float32)]
    select_n x2 -> x0, other arithmetic: 5.61 us -> none  [spread(): return lax.psum(jnp.where(mine, shard, jnp.zeros_like(shard)), axis)]
    unnamed x13 -> x10, local copies, waits for them, and re-layouts: 1.17 us -> 5.79 us
  transfers between devices with their start and end apart: 2 -> 0, of which waited for: 2 -> 0; matrix products, arithmetic and copies ran while one was open for 1% -> 0% of each run, Pallas kernels for 0% -> 0%
where the time goes in v2:
time: 84.4 us; the launch traced here: 84.2 us
  Pallas kernels  78.3 us (93%)
  local copies, waits for them, and re-layouts  5.79 us (7%)
    pallas_call x1, Pallas kernels, per_device(): pl.pallas_call(comm_kernel, out_shape=[jax.ShapeDtypeStruct((2, SB_R, 2,...  63.9 us
    pallas_call x1, Pallas kernels, per_device(): pl.pallas_call(product_kernel, out_shape=jax.ShapeDtypeStruct((n, LC * BS...  14.4 us
    unnamed x10, local copies, waits for them, and re-layouts  5.79 us

profile of v2, /device:TPU:1, one launch (start us, length us, event | category | flops | bytes accessed | tf_op | source)
XLA Modules:
  0.0 84.2 jit_solution(14910279083515076638)
XLA Ops:
  0.0 0.1 pad_add_fusion.here
  0.1 0.0 copy-start
  0.1 1.0 %copy-done = bf16[16,128,128]{2,1,0:T(8,128)(2,1)S(1)} copy-done((bf16[16,128,128]{2,1,0:T(8,128)(2,1)S(1)}, bf16[16,128,128]{2,1,0:T(8,128)(2,1)}, u32[]{:S(2)}) %copy-start) | copy-done | bytes 524312
  1.1 0.0 copy-start.1
  1.1 0.7 copy-done.1
  1.8 0.0 copy-start.2
  1.8 0.7 copy-done.2
  2.4 63.9 %spread_tiles.1 = (bf16[2,52,2,4,32,128]{5,4,3,2,1,0:T(8,128)(2,1)S(1)}, bf16[2,24,4,64,128]{4,3,2,1,0:T(8,128)(2,1)S(1)}, s32[2,8,128]{2,1,0:T(8,128)S(1)}) custom-call(s32[4]{0:T(128)S(1)} %copy-done.2, s32[1,16]{1,0:T(1,128)S(1)} %copy-done.1, bf16[16,128,128]{2,1,0:T(8,128)(2,1)S(1)} %copy-done), custom_call_target="tpu_custom_call" | custom-call | tf_op jit(solution)/shard_map/spread_tiles/pallas_call | solution.py:365
  66.4 0.0 copy-start.4
  66.4 2.8 %copy-done.4 = bf16[2,52,2,4,32,128]{5,4,3,2,1,0:T(8,128)(2,1)} copy-done((bf16[2,52,2,4,32,128]{5,4,3,2,1,0:T(8,128)(2,1)}, bf16[2,52,2,4,32,128]{5,4,3,2,1,0:T(8,128)(2,1)S(1)}, u32[]{:S(2)}) %copy-start.4) | copy-done | bytes 6815768
  69.2 0.0 copy-start.3
  69.2 0.7 copy-done.3
  69.8 14.4 %panel_product.1 = f32[1024,1024]{1,0:T(8,128)} custom-call(s32[4]{0:T(128)S(1)} %copy-done.3, s32[2]{0:T(128)S(1)} %pad_add_fusion.here, s32[2,8,128]{2,1,0:T(8,128)S(1)} %get-tuple-element.8.meta, bf16[2,52,2,4,32,128]{5,4,3,2,1,0:T(8,128)(2,1)} %copy-done.4, bf16[2,24,4,64,128]{4,3,2,1,0:T(8,128)(2,1)S(1)} %get-tuple-element.10.sa), custom_call_target="tpu_custom_call" | custom-call | flops 4294967296 | bytes 10485760 | tf_op jit(solution)/shard_map/panel_product/pallas_call | solution.py:397
Async XLA Ops:
  0.1 1.0 %copy-start = (bf16[16,128,128]{2,1,0:T(8,128)(2,1)S(1)}, bf16[16,128,128]{2,1,0:T(8,128)(2,1)}, u32[]{:S(2)}) copy-start(bf16[16,128,128]{2,1,0:T(8,128)(2,1)} %x_hbm.1) | copy-start | bytes 1572868
  1.1 0.7 copy-start.1
  1.8 0.7 copy-start.2
  66.4 2.8 %copy-start.4 = (bf16[2,52,2,4,32,128]{5,4,3,2,1,0:T(8,128)(2,1)}, bf16[2,52,2,4,32,128]{5,4,3,2,1,0:T(8,128)(2,1)S(1)}, u32[]{:S(2)}) copy-start(bf16[2,52,2,4,32,128]{5,4,3,2,1,0:T(8,128)(2,1)S(1)} %get-tuple-element.9.sb) | copy-start | bytes 20447236
  69.2 0.7 copy-start.3

commit v3 on v2

v3 whole, which is shorter than its diff:
```python
import jax
import jax.numpy as jnp
from jax import lax
from jax.experimental import pallas as pl
from jax.experimental.pallas import tpu as pltpu
from jax.sharding import PartitionSpec as P

BS = 128
LR = 8
LC = 8
PW = 4
SECTIONS = 4
SLOTS = 16
WIN = 12
HALF = WIN // 2
LOW = SLOTS - WIN
NZ, NX = 8, 4
CB, CA = 16, 32
MB, MA = 7, 5
QB, QA = BS // CB, BS // CA
NB_R, NA_R = HALF * QB, HALF * QA
NRING = 8
TB_R, TA_R = NB_R + (NRING - 2) * MB, NA_R + (NRING - 2) * MA
SB_R, SA_R = TB_R + MB, TA_R + MA
MESH = pl.DeviceIdType.MESH

HANDED = [
    [(s, 0, 64) for s in (0, 4, 6, 10)],
    [(s, 64, 64) for s in (0, 4, 6, 10)],
    [(s, 0, BS) for s in (1, 5, 7, 11)],
    [(s, 0, BS) for s in (2, 8, 12)],
    [(s, 0, BS) for s in (3, 9, 13)],
    [(14, 0, BS)],
    [(15, 0, BS)],
]
PIECES = [piece for group in HANDED for piece in group]


def comm_kernel(
    panels_hbm, pos_hbm, x_hbm, sb, sa, meta,
    panels, pos, xv, xa, pc, rb, ra, mo, mc, mb, mt,
    x_sem, i_sem, h_send, h_recv, b_send, b_recv, a_send, a_recv, s_send, s_recv,
    mh_send, mh_recv, mr_send, mr_recv, mf_send, mf_recv,
):
    row = lax.axis_index("row")
    col = lax.axis_index("col")
    core = lax.rem(col, 2)
    z, yh = lax.rem(row, NZ), row // NZ
    x, yl = lax.rem(col // 2, NX), col // 8
    place = jnp.where(yl == 0, x, NRING - 1 - x)

    def dev(zz, yyh, xx, yyl, cc):
        return {"row": yyh * NZ + zz, "col": (yyl * NX + xx) * 2 + cc}

    def around(step):
        p = lax.rem(place + step, NRING)
        back = p // NX
        return dev(z, yh, jnp.where(back == 0, p, NRING - 1 - p), back, core)

    z_to = [dev(lax.rem(z + 1, NZ), yh, x, yl, core), dev(lax.rem(z + NZ - 1, NZ), yh, x, yl, core)]
    x_to = [around(1), around(NRING - 1)]
    sibling = dev(z, yh, x, yl, 1 - core)
    yh_same, yh_cross = dev(z, 1 - yh, x, yl, core), dev(z, 1 - yh, x, yl, 1 - core)

    def remote(src, dst, send, recv, to):
        return pltpu.make_async_remote_copy(
            src_ref=src, dst_ref=dst, send_sem=send, recv_sem=recv,
            device_id=to, device_id_type=MESH)

    fetch = [
        pltpu.make_async_copy(x_hbm, xv, x_sem),
        pltpu.make_async_copy(panels_hbm, panels, i_sem.at[0]),
        pltpu.make_async_copy(pos_hbm, pos, i_sem.at[1]),
    ]
    for f in fetch:
        f.start()
    barrier = pltpu.get_barrier_semaphore()

    def greet(peers):
        for peer in peers:
            pl.semaphore_signal(barrier, inc=1, device_id=peer, device_id_type=MESH)
        pl.semaphore_wait(barrier, len(peers))
        fetch[0].wait()

    lane = lax.broadcasted_iota(jnp.int32, (8, BS), 1)
    sub = lax.broadcasted_iota(jnp.int32, (8, BS), 0)

    def hand(source, to, j, n):
        s, r, rows = PIECES[n]
        at = (s, pl.ds(r, rows))
        return remote(
            source.at[at], pc.at[(j, *at)], h_send.at[j], h_recv.at[j, n], to)

    def hand_meta(to, j):
        return remote(mo, mc.at[j], mh_send.at[j], mh_recv.at[j], to)

    def hand_over(source, to, j, groups=range(len(HANDED))):
        for g in groups:
            for piece in HANDED[g]:
                hand(source, to, j, PIECES.index(piece)).start()

    def handed(g, js):
        for piece in HANDED[g]:
            for j in js:
                hand(xv, sibling, j, PIECES.index(piece)).wait_recv()

    def all_left(ref, sem):
        pltpu.make_async_copy(ref, ref, sem).wait()

    def pick(own, low_high, cond, v):
        return lax.select(cond, lax.select(own, low_high[1], low_high[0]), v)

    def sort():
        fetch[1].wait()
        fetch[2].wait()
        spot = [pos[0, s] for s in range(SLOTS)]
        right = [lax.rem(p, LC) // PW for p in spot]
        lefts, rights, rank = 0, SLOTS - sum(right), []
        for s in range(SLOTS):
            rank.append(jnp.where(right[s] == 0, lefts, rights))
            lefts, rights = lefts + 1 - right[s], rights + right[s]
        where = jnp.zeros((8, BS), jnp.int32)
        for s in range(SLOTS):
            where = jnp.where((sub == 0) & (lane == s), spot[s], where)
            where = jnp.where((sub == 1) & (lane == rank[s]), spot[s], where)
        mo[...] = where
        for i in range(SLOTS):
            src = sum(jnp.where(rank[s] == i, s, 0) for s in range(SLOTS))
            xa[i] = xv[src]

    def ring_meta(j, to):
        return remote(mb.at[j], mb.at[j + 1], mr_send, mr_recv.at[j], to)

    def finish_meta(part, rows, far, high, unit):
        for k in range(SECTIONS):
            hops = mb[far[k]]
            for cc in range(2):
                line = hops[rows[cc] + k : rows[cc] + k + 1, :]
                lanes = lane[0:1, :]
                line = jnp.where(lanes == SLOTS, jnp.where(high[k], LOW, 0), line)
                line = jnp.where(lanes == SLOTS + 1, far[k] * unit, line)
                line = jnp.where(lanes == SLOTS + 2, lax.rem(NRING - far[k], NRING) * unit, line)
                line = jnp.where(lanes == SLOTS + 3, cc, line)
                line = jnp.where(lanes == SLOTS + 4, jnp.where(high[k], 1, 0), line)
                out = meta.at[part] if part == 1 - cc else mt
                out[k : k + 1, :] = line
        remote(mt, meta.at[part], mf_send, mf_recv, sibling).start()

    def b_copy(d, t):
        return remote(sb.at[d, t], rb.at[d, t], b_send.at[d], b_recv.at[d, t], z_to[d])

    def b_share(d, t):
        return remote(sb.at[d, t, 0], sb.at[d, t, 0], s_send.at[d], s_recv.at[d], sibling)

    @pl.when(core == 1)
    def _():
        greet(z_to + [sibling, yh_same, yh_cross])
        hand_over(xv, yh_same, 1, (0, 1))
        sort()
        owner = [panels[k] // 2 for k in range(SECTIONS)]
        high = [lax.rem(panels[k], 2) == 1 for k in range(SECTIONS)]
        hand_meta(yh_same, 1).start()
        hand_meta(sibling, 0).start()
        hand_over(xa, sibling, 0)
        own_here = [owner[k] == row for k in range(SECTIONS)]
        own_there = [owner[k] == (1 - yh) * NZ + z for k in range(SECTIONS)]

        def b_round(t, i, q, first):
            rows = pl.ds(q * CB, CB)
            for d in range(2):
                s0 = i + HALF * d
                if not first:
                    b_copy(d, t - MB).wait_recv()
                for cc in range(2):
                    if cc == 1:
                        here = [xv[s, rows, :] for s in (s0, s0 + LOW)]
                    else:
                        here = [pc[0, s, rows, :] for s in (s0, s0 + LOW)]
                    there = [pc[2 - cc, s, rows, :] for s in (s0, s0 + LOW)]
                    for k in range(SECTIONS):
                        v = here[0] if first else rb[d, t - MB, cc, k]
                        v = pick(high[k], there, own_there[k], v)
                        v = pick(high[k], here, own_here[k], v)
                        sb[d, t, cc, k] = v
                b_copy(d, t).start()
                b_share(d, t).start()

        for i in range(HALF):
            handed(i + (i > 0), (0, 1, 2))
            hand_over(xv, yh_same, 1, ((2,), (4,), (5, 6))[i] if i < 3 else ())
            if i * QB < MB:
                for q in range(QB):
                    if i == 0 and q == QB // 2:
                        handed(1, (0, 1, 2))
                        hand_over(xv, yh_same, 1, (3,))
                    b_round(i * QB + q, i, q, i * QB + q < MB)
            else:
                def step(q, _, i=i):
                    b_round(i * QB + q, i, q, False)
                    return 0

                lax.fori_loop(0, QB, step, 0)
            if i == 0:
                for j in range(3):
                    hand_meta(sibling, j).wait_recv()
                for cc in range(2):
                    here = mo[0:1, :] if cc == 1 else mc[0, 0:1, :]
                    there = mc[2 - cc, 0:1, :]
                    for k in range(SECTIONS):
                        r = cc * SECTIONS + k
                        mb[0, r : r + 1, :] = jnp.where(own_here[k], here, there)
            else:
                ring_meta(i - 1, z_to[0]).wait_recv()
            ring_meta(i, z_to[0]).start()

        def tail(t, _):
            for d in range(2):
                b_copy(d, t - MB).wait_recv()
                sb[d, t] = rb[d, t - MB]

                @pl.when(t < TB_R)
                def _():
                    b_copy(d, t).start()

                b_share(d, t).start()
            return 0

        lax.fori_loop(NB_R, NB_R + MB, tail, 0)
        ring_meta(HALF - 1, z_to[0]).wait_recv()
        ring_meta(HALF, z_to[0]).start()
        lax.fori_loop(NB_R + MB, NB_R + 5 * MB, tail, 0)
        ring_meta(HALF, z_to[0]).wait_recv()
        far = [lax.rem(z - lax.rem(owner[k], NZ) + NZ, NZ) for k in range(SECTIONS)]
        finish_meta(0, (0, SECTIONS), far, high, MB)
        lax.fori_loop(NB_R + 5 * MB, SB_R, tail, 0)
        for d in range(2):
            all_left(sb.at[d, pl.ds(0, TB_R)], b_send.at[d])
            all_left(sb.at[d, pl.ds(0, SB_R), 0], s_send.at[d])
            all_left(sa.at[d], s_recv.at[d])
        for j in (0, 1):
            all_left(pc.at[j], h_send.at[j])
            all_left(mo, mh_send.at[j])

    def a_copy(d, t):
        return remote(sa.at[d, t], ra.at[d, t], a_send.at[d], a_recv.at[d, t], x_to[d])

    def a_share(d, t):
        return remote(sa.at[d, t], sa.at[d, t], s_send.at[d], s_recv.at[d], sibling)

    @pl.when(core == 0)
    def _():
        greet(x_to + [sibling, yh_cross])
        hand_over(xv, yh_cross, 2, (0, 1))
        hand_over(xv, sibling, 0)
        sort()
        owner = [panels[k] // 2 for k in range(SECTIONS)]
        high = [lax.rem(panels[k], 2) == 1 for k in range(SECTIONS)]
        hand_meta(yh_cross, 2).start()
        hand_meta(sibling, 0).start()
        own_here = [owner[k] == col for k in range(SECTIONS)]
        own_there = [owner[k] == col + 1 for k in range(SECTIONS)]

        def a_round(t, i, q, first):
            rows = pl.ds(q * CA, CA)
            for d in range(2):
                s0 = i + HALF * d
                if not first:
                    a_copy(d, t - MA).wait_recv()
                here = [xa[s, rows, :] for s in (s0, s0 + LOW)]
                there = [pc[0, s, rows, :] for s in (s0, s0 + LOW)]
                for k in range(SECTIONS):
                    v = here[0] if first else ra[d, t - MA, k]
                    v = pick(high[k], there, own_there[k], v)
                    v = pick(high[k], here, own_here[k], v)
                    sa[d, t, k] = v
                a_copy(d, t).start()
                a_share(d, t).start()

        for i in range(HALF):
            handed(i + (i > 0), (0,))
            hand_over(xv, yh_cross, 2, ((2,), (4,), (5, 6))[i] if i < 3 else ())
            if i * QA < MA:
                for q in range(QA):
                    if i == 0 and q == QA // 2:
                        handed(1, (0,))
                        hand_over(xv, yh_cross, 2, (3,))
                    a_round(i * QA + q, i, q, i * QA + q < MA)
            else:
                def step(q, _, i=i):
                    a_round(i * QA + q, i, q, False)
                    return 0

                lax.fori_loop(0, QA, step, 0)
            if i == 0:
                hand_meta(sibling, 0).wait_recv()
                for k in range(SECTIONS):
                    mb[0, k : k + 1, :] = jnp.where(own_here[k], mo[1:2, :], mc[0, 1:2, :])
                    mb[0, SECTIONS + k : SECTIONS + k + 1, :] = mo[0:1, :]
            else:
                ring_meta(i - 1, x_to[0]).wait_recv()
            ring_meta(i, x_to[0]).start()

        def tail(t, _):
            for d in range(2):
                a_copy(d, t - MA).wait_recv()
                sa[d, t] = ra[d, t - MA]

                @pl.when(t < TA_R)
                def _():
                    a_copy(d, t).start()

                a_share(d, t).start()
            return 0

        lax.fori_loop(NA_R, NA_R + MA, tail, 0)
        ring_meta(HALF - 1, x_to[0]).wait_recv()
        ring_meta(HALF, x_to[0]).start()
        lax.fori_loop(NA_R + MA, NA_R + 5 * MA, tail, 0)
        ring_meta(HALF, x_to[0]).wait_recv()
        far = []
        for k in range(SECTIONS):
            xo, yo = lax.rem(owner[k] // 2, NX), owner[k] // 8
            far.append(lax.rem(place - jnp.where(yo == 0, xo, NRING - 1 - xo) + NRING, NRING))
        finish_meta(1, (0, 0), far, high, MA)
        lax.fori_loop(NA_R + 5 * MA, SA_R, tail, 0)
        for d in range(2):
            all_left(sa.at[d, pl.ds(0, TA_R)], a_send.at[d])
            all_left(sa.at[d], s_send.at[d])
            all_left(sb.at[d, pl.ds(0, SB_R), 0], s_recv.at[d])
        for j in (0, 2):
            all_left(pc.at[j], h_send.at[j])
            all_left(mo, mh_send.at[j])

    all_left(mb.at[pl.ds(0, NRING - 1)], mr_send)
    all_left(mt, mf_send)
    all_left(mt, mf_recv)


def product_kernel(meta, sb, sa, c_ref, a_full, b_full):
    @pl.when(pl.program_id(0) == 0)
    def _():
        a_full[...] = jnp.zeros_like(a_full)
        b_full[...] = jnp.zeros_like(b_full)

        def section(k, _):
            for part in range(2):
                low = meta[part, k, SLOTS]
                start = [meta[part, k, SLOTS + 1], meta[part, k, SLOTS + 2]]
                core = meta[part, k, SLOTS + 3]
                high = meta[part, k, SLOTS + 4]
                for w in range(WIN):
                    p = meta[part, k, low + w]
                    d = w // HALF
                    if part == 0:
                        @pl.when((p >> 5) == high)
                        def _(p=p, d=d, w=w, start=start, core=core):
                            v = sb[d, pl.ds(start[d] + (w % HALF) * QB, QB), core, k]
                            r0 = pl.multiple_of((k * PW + ((p >> 3) & 3)) * BS, BS)
                            c0 = pl.multiple_of((p & 7) * BS, BS)
                            b_full[pl.ds(r0, BS), pl.ds(c0, BS)] = v.reshape(BS, BS)
                    else:
                        @pl.when(((p >> 2) & 1) == high)
                        def _(p=p, d=d, w=w, start=start):
                            v = sa[d, pl.ds(start[d] + (w % HALF) * QA, QA), k]
                            r0 = pl.multiple_of((p >> 3) * BS, BS)
                            c0 = pl.multiple_of((k * PW + (p & 3)) * BS, BS)
                            a_full[pl.ds(r0, BS), pl.ds(c0, BS)] = v.reshape(BS, BS)
            return 0

        lax.fori_loop(0, SECTIONS, section, 0)

    rows = c_ref.shape[0]
    r0 = pl.multiple_of(pl.program_id(0) * rows, rows)
    c_ref[...] = jnp.dot(
        a_full[pl.ds(r0, rows), :], b_full[...], preferred_element_type=jnp.float32)


def per_device(x_tiles, tile_pos, panel_ids):
    vmem = pl.BlockSpec(memory_space=pltpu.VMEM)
    smem = pl.BlockSpec(memory_space=pltpu.SMEM)
    hbm = pl.BlockSpec(memory_space=pltpu.HBM)
    bf16, i32 = jnp.bfloat16, jnp.int32
    dma = pltpu.SemaphoreType.DMA
    sb, sa, meta = pl.pallas_call(
        comm_kernel,
        out_shape=[
            jax.ShapeDtypeStruct((2, SB_R, 2, SECTIONS, CB, BS), bf16),
            jax.ShapeDtypeStruct((2, SA_R, SECTIONS, CA, BS), bf16),
            jax.ShapeDtypeStruct((2, 8, BS), i32),
        ],
        in_specs=[hbm, hbm, hbm],
        out_specs=[vmem, vmem, vmem],
        scratch_shapes=[
            pltpu.SMEM((SECTIONS,), i32),
            pltpu.SMEM((1, SLOTS), i32),
            pltpu.VMEM((SLOTS, BS, BS), bf16),
            pltpu.VMEM((SLOTS, BS, BS), bf16),
            pltpu.VMEM((3, SLOTS, BS, BS), bf16),
            pltpu.VMEM((2, TB_R, 2, SECTIONS, CB, BS), bf16),
            pltpu.VMEM((2, TA_R, SECTIONS, CA, BS), bf16),
            pltpu.VMEM((8, BS), i32),
            pltpu.VMEM((3, 8, BS), i32),
            pltpu.VMEM((NRING, 8, BS), i32),
            pltpu.VMEM((8, BS), i32),
            dma, dma((2,)), dma((3,)), dma((3, len(PIECES))),
            dma((2,)), dma((2, TB_R)), dma((2,)), dma((2, TA_R)), dma((2,)), dma((2,)),
            dma((3,)), dma((3,)), dma, dma((NRING - 1,)), dma, dma,
        ],
        compiler_params=pltpu.CompilerParams(
            collective_id=0, has_side_effects=True, vmem_limit_bytes=28 << 20),
        name="spread_tiles",
    )(*[
        pltpu.with_memory_space_constraint(v, pltpu.HBM)
        for v in (panel_ids, tile_pos, x_tiles)
    ])
    n = LR * BS
    kdim = SECTIONS * PW * BS
    steps = 4
    return pl.pallas_call(
        product_kernel,
        out_shape=jax.ShapeDtypeStruct((n, LC * BS), jnp.float32),
        grid=(steps,),
        in_specs=[smem, vmem, vmem],
        out_specs=pl.BlockSpec((n // steps, LC * BS), lambda i: (i, 0)),
        scratch_shapes=[pltpu.VMEM((n, kdim), bf16), pltpu.VMEM((kdim, LC * BS), bf16)],
        compiler_params=pltpu.CompilerParams(vmem_limit_bytes=16 << 20),
        cost_estimate=pl.CostEstimate(
            flops=2 * n * kdim * LC * BS, bytes_accessed=10 << 20, transcendentals=0),
        name="panel_product",
    )(meta, sb, sa)


def solution(mesh):
    in_specs = (P("row", "col", None), P("row", "col"), P())
    out_specs = P("row", "col")
    return jax.shard_map(
        per_device, mesh=mesh, in_specs=in_specs, out_specs=out_specs, check_vma=False
    )
```

time: 84.4 us -> 62.3 us (0.74)
  Pallas kernels: 78.3 us -> 62.2 us
  local copies, waits for them, and re-layouts: 5.79 us -> 0 us
    pallas_call x1, Pallas kernels: 63.9 us -> 53.5 us  [per_device(): pl.pallas_call(comm_kernel, out_shape=[jax.ShapeDtypeStruct((2, SB_R, 2,...]
    unnamed x10 -> x0, local copies, waits for them, and re-layouts: 5.79 us -> none
    pallas_call x1, Pallas kernels: 14.4 us -> 8.77 us  [per_device(): pl.pallas_call(product_kernel, out_shape=jax.ShapeDtypeStruct((n, LC * BS...]
where the time goes in v3:
time: 62.3 us
  Pallas kernels  62.2 us (100%)
    pallas_call x1, Pallas kernels, per_device(): pl.pallas_call(comm_kernel, out_shape=[jax.ShapeDtypeStruct((2, SB_R, 2,...  53.5 us
    pallas_call x1, Pallas kernels, per_device(): pl.pallas_call(product_kernel, out_shape=jax.ShapeDtypeStruct((n, LC * BS...  8.77 us

profile of v3, /device:TPU:1, one launch (start us, length us, event | category | flops | bytes accessed | tf_op | source)
XLA Modules:
  0.0 62.3 jit_solution(2180616216739992619)
XLA Ops:
  0.0 53.5 %spread_tiles.1 = (bf16[2,97,2,4,16,128]{5,4,3,2,1,0:T(8,128)(2,1)S(1)}, bf16[2,59,4,32,128]{4,3,2,1,0:T(8,128)(2,1)S(1)}, s32[2,8,128]{2,1,0:T(8,128)S(1)}) custom-call(s32[4]{0:T(128)} %panels_hbm.1, s32[1,16]{1,0:T(1,128)} %pos_hbm.1, bf16[16,128,128]{2,1,0:T(8,128)(2,1)} %x_hbm.1), custom_call_target="tpu_custom_call" | custom-call | tf_op jit(solution)/shard_map/spread_tiles/pallas_call | solution.py:384
  53.5 8.8 %panel_product.1 = f32[1024,1024]{1,0:T(8,128)} custom-call(s32[2,8,128]{2,1,0:T(8,128)S(1)} %get-tuple-element.8.meta, bf16[2,97,2,4,16,128]{5,4,3,2,1,0:T(8,128)(2,1)S(1)} %get-tuple-element.9.sb, bf16[2,59,4,32,128]{4,3,2,1,0:T(8,128)(2,1)S(1)} %get-tuple-element.10.sa), custom_call_target="tpu_custom_call" | custom-call | flops 4294967296 | bytes 10485760 | tf_op jit(solution)/shard_map/panel_product/pallas_call | solution.py:419

commit v4 on v3

--- a/solution.py
+++ b/solution.py
@@ -24,15 +24,20 @@
 SB_R, SA_R = TB_R + MB, TA_R + MA
 MESH = pl.DeviceIdType.MESH
 
+def slots_of(i, d):
+    if i < (WIN - LOW) // 2:
+        return [LOW + 2 * i + d]
+    s = 2 * (i - (WIN - LOW) // 2) + d
+    return [s, WIN + s]
+
+
+FIRST = 32
 HANDED = [
-    [(s, 0, 64) for s in (0, 4, 6, 10)],
-    [(s, 64, 64) for s in (0, 4, 6, 10)],
-    [(s, 0, BS) for s in (1, 5, 7, 11)],
-    [(s, 0, BS) for s in (2, 8, 12)],
-    [(s, 0, BS) for s in (3, 9, 13)],
-    [(14, 0, BS)],
-    [(15, 0, BS)],
+    [(s, 0, FIRST) for d in range(2) for s in slots_of(0, d)],
+    [(s, FIRST, BS - FIRST) for d in range(2) for s in slots_of(0, d)],
 ]
+for _i in range(1, HALF):
+    HANDED.append([(s, 0, BS) for d in range(2) for s in slots_of(_i, d)])
 PIECES = [piece for group in HANDED for piece in group]
 
 
@@ -108,7 +113,10 @@
         pltpu.make_async_copy(ref, ref, sem).wait()
 
     def pick(own, low_high, cond, v):
-        return lax.select(cond, lax.select(own, low_high[1], low_high[0]), v)
+        mine = low_high[0]
+        if len(low_high) == 2:
+            mine = lax.select(own, low_high[1], mine)
+        return lax.select(cond, mine, v)
 
     def sort():
         fetch[1].wait()
@@ -137,7 +145,7 @@
             for cc in range(2):
                 line = hops[rows[cc] + k : rows[cc] + k + 1, :]
                 lanes = lane[0:1, :]
-                line = jnp.where(lanes == SLOTS, jnp.where(high[k], LOW, 0), line)
+                line = jnp.where(lanes == SLOTS, jnp.where(high[k], WIN, 0), line)
                 line = jnp.where(lanes == SLOTS + 1, far[k] * unit, line)
                 line = jnp.where(lanes == SLOTS + 2, lax.rem(NRING - far[k], NRING) * unit, line)
                 line = jnp.where(lanes == SLOTS + 3, cc, line)
@@ -155,7 +163,7 @@
     @pl.when(core == 1)
     def _():
         greet(z_to + [sibling, yh_same, yh_cross])
-        hand_over(xv, yh_same, 1, (0, 1))
+        hand_over(xv, yh_same, 1, (0, 1, 2))
         sort()
         owner = [panels[k] // 2 for k in range(SECTIONS)]
         high = [lax.rem(panels[k], 2) == 1 for k in range(SECTIONS)]
@@ -168,15 +176,15 @@
         def b_round(t, i, q, first):
             rows = pl.ds(q * CB, CB)
             for d in range(2):
-                s0 = i + HALF * d
+                slots = slots_of(i, d)
                 if not first:
                     b_copy(d, t - MB).wait_recv()
                 for cc in range(2):
                     if cc == 1:
-                        here = [xv[s, rows, :] for s in (s0, s0 + LOW)]
+                        here = [xv[s, rows, :] for s in slots]
                     else:
-                        here = [pc[0, s, rows, :] for s in (s0, s0 + LOW)]
-                    there = [pc[2 - cc, s, rows, :] for s in (s0, s0 + LOW)]
+                        here = [pc[0, s, rows, :] for s in slots]
+                    there = [pc[2 - cc, s, rows, :] for s in slots]
                     for k in range(SECTIONS):
                         v = here[0] if first else rb[d, t - MB, cc, k]
                         v = pick(high[k], there, own_there[k], v)
@@ -187,12 +195,12 @@
 
         for i in range(HALF):
             handed(i + (i > 0), (0, 1, 2))
-            hand_over(xv, yh_same, 1, ((2,), (4,), (5, 6))[i] if i < 3 else ())
+            hand_over(xv, yh_same, 1, ((3,), (5,), (6,))[i] if i < 3 else ())
             if i * QB < MB:
                 for q in range(QB):
-                    if i == 0 and q == QB // 2:
+                    if i == 0 and q == FIRST // CB:
                         handed(1, (0, 1, 2))
-                        hand_over(xv, yh_same, 1, (3,))
+                        hand_over(xv, yh_same, 1, (4,))
                     b_round(i * QB + q, i, q, i * QB + q < MB)
             else:
                 def step(q, _, i=i):
@@ -250,7 +258,7 @@
     @pl.when(core == 0)
     def _():
         greet(x_to + [sibling, yh_cross])
-        hand_over(xv, yh_cross, 2, (0, 1))
+        hand_over(xv, yh_cross, 2, (0, 1, 2))
         hand_over(xv, sibling, 0)
         sort()
         owner = [panels[k] // 2 for k in range(SECTIONS)]
@@ -263,11 +271,11 @@
         def a_round(t, i, q, first):
             rows = pl.ds(q * CA, CA)
             for d in range(2):
-                s0 = i + HALF * d
+                slots = slots_of(i, d)
                 if not first:
                     a_copy(d, t - MA).wait_recv()
-                here = [xa[s, rows, :] for s in (s0, s0 + LOW)]
-                there = [pc[0, s, rows, :] for s in (s0, s0 + LOW)]
+                here = [xa[s, rows, :] for s in slots]
+                there = [pc[0, s, rows, :] for s in slots]
                 for k in range(SECTIONS):
                     v = here[0] if first else ra[d, t - MA, k]
                     v = pick(high[k], there, own_there[k], v)
@@ -278,12 +286,12 @@
 
         for i in range(HALF):
             handed(i + (i > 0), (0,))
-            hand_over(xv, yh_cross, 2, ((2,), (4,), (5, 6))[i] if i < 3 else ())
+            hand_over(xv, yh_cross, 2, ((3,), (5,), (6,))[i] if i < 3 else ())
             if i * QA < MA:
                 for q in range(QA):
-                    if i == 0 and q == QA // 2:
+                    if i == 0 and q == FIRST // CA:
                         handed(1, (0,))
-                        hand_over(xv, yh_cross, 2, (3,))
+                        hand_over(xv, yh_cross, 2, (4,))
                     a_round(i * QA + q, i, q, i * QA + q < MA)
             else:
                 def step(q, _, i=i):
@@ -344,13 +352,14 @@
 
         def section(k, _):
             for part in range(2):
-                low = meta[part, k, SLOTS]
+                late = meta[part, k, SLOTS]
                 start = [meta[part, k, SLOTS + 1], meta[part, k, SLOTS + 2]]
                 core = meta[part, k, SLOTS + 3]
                 high = meta[part, k, SLOTS + 4]
                 for w in range(WIN):
-                    p = meta[part, k, low + w]
                     d = w // HALF
+                    slots = slots_of(w % HALF, d)
+                    p = meta[part, k, slots[0] + (late if len(slots) == 2 else 0)]
                     if part == 0:
                         @pl.when((p >> 5) == high)
                         def _(p=p, d=d, w=w, start=start, core=core):

time: 62.3 us -> 61.6 us (0.989)
  Pallas kernels: 62.2 us -> 61.5 us
    pallas_call x1, Pallas kernels: 53.5 us -> 52.7 us  [per_device(): pl.pallas_call(comm_kernel, out_shape=[jax.ShapeDtypeStruct((2, SB_R, 2,...]
where the time goes in v4:
time: 61.6 us; the launch traced here: 61.5 us
  Pallas kernels  61.5 us (100%)
    pallas_call x1, Pallas kernels, per_device(): pl.pallas_call(comm_kernel, out_shape=[jax.ShapeDtypeStruct((2, SB_R, 2,...  52.7 us
    pallas_call x1, Pallas kernels, per_device(): pl.pallas_call(product_kernel, out_shape=jax.ShapeDtypeStruct((n, LC * BS...  8.76 us

profile of v4, /device:TPU:1, one launch (start us, length us, event | category | flops | bytes accessed | tf_op | source)
XLA Modules:
  0.0 61.5 jit_solution(589539689211387628)
XLA Ops:
  0.0 52.7 %spread_tiles.1 = (bf16[2,97,2,4,16,128]{5,4,3,2,1,0:T(8,128)(2,1)S(1)}, bf16[2,59,4,32,128]{4,3,2,1,0:T(8,128)(2,1)S(1)}, s32[2,8,128]{2,1,0:T(8,128)S(1)}) custom-call(s32[4]{0:T(128)} %panels_hbm.1, s32[1,16]{1,0:T(1,128)} %pos_hbm.1, bf16[16,128,128]{2,1,0:T(8,128)(2,1)} %x_hbm.1), custom_call_target="tpu_custom_call" | custom-call | tf_op jit(solution)/shard_map/spread_tiles/pallas_call | solution.py:393
  52.7 8.8 %panel_product.1 = f32[1024,1024]{1,0:T(8,128)} custom-call(s32[2,8,128]{2,1,0:T(8,128)S(1)} %get-tuple-element.8.meta, bf16[2,97,2,4,16,128]{5,4,3,2,1,0:T(8,128)(2,1)S(1)} %get-tuple-element.9.sb, bf16[2,59,4,32,128]{4,3,2,1,0:T(8,128)(2,1)S(1)} %get-tuple-element.10.sa), custom_call_target="tpu_custom_call" | custom-call | flops 4294967296 | bytes 10485760 | tf_op jit(solution)/shard_map/panel_product/pallas_call | solution.py:428

commit v5 on v4

--- a/solution.py
+++ b/solution.py
@@ -191,6 +191,7 @@
                         v = pick(high[k], here, own_here[k], v)
                         sb[d, t, cc, k] = v
                 b_copy(d, t).start()
+            for d in range(2):
                 b_share(d, t).start()
 
         for i in range(HALF):
@@ -230,6 +231,7 @@
                 def _():
                     b_copy(d, t).start()
 
+            for d in range(2):
                 b_share(d, t).start()
             return 0
 
@@ -282,6 +284,7 @@
                     v = pick(high[k], here, own_here[k], v)
                     sa[d, t, k] = v
                 a_copy(d, t).start()
+            for d in range(2):
                 a_share(d, t).start()
 
         for i in range(HALF):
@@ -317,6 +320,7 @@
                 def _():
                     a_copy(d, t).start()
 
+            for d in range(2):
                 a_share(d, t).start()
             return 0
 

time: 61.6 us -> 61.7 us (level)
  no operation moved by 1% of the time
where the time goes in v5:
time: 61.7 us; the launch traced here: 61.5 us
  Pallas kernels  61.5 us (100%)
    pallas_call x1, Pallas kernels, per_device(): pl.pallas_call(comm_kernel, out_shape=[jax.ShapeDtypeStruct((2, SB_R, 2,...  52.8 us
    pallas_call x1, Pallas kernels, per_device(): pl.pallas_call(product_kernel, out_shape=jax.ShapeDtypeStruct((n, LC * BS...  8.76 us

profile of v5, /device:TPU:1, one launch (start us, length us, event | category | flops | bytes accessed | tf_op | source)
XLA Modules:
  0.0 61.5 jit_solution(14575335057082900657)
XLA Ops:
  0.0 52.8 %spread_tiles.1 = (bf16[2,97,2,4,16,128]{5,4,3,2,1,0:T(8,128)(2,1)S(1)}, bf16[2,59,4,32,128]{4,3,2,1,0:T(8,128)(2,1)S(1)}, s32[2,8,128]{2,1,0:T(8,128)S(1)}) custom-call(s32[4]{0:T(128)} %panels_hbm.1, s32[1,16]{1,0:T(1,128)} %pos_hbm.1, bf16[16,128,128]{2,1,0:T(8,128)(2,1)} %x_hbm.1), custom_call_target="tpu_custom_call" | custom-call | tf_op jit(solution)/shard_map/spread_tiles/pallas_call | solution.py:397
  52.8 8.8 %panel_product.1 = f32[1024,1024]{1,0:T(8,128)} custom-call(s32[2,8,128]{2,1,0:T(8,128)S(1)} %get-tuple-element.8.meta, bf16[2,97,2,4,16,128]{5,4,3,2,1,0:T(8,128)(2,1)S(1)} %get-tuple-element.9.sb, bf16[2,59,4,32,128]{4,3,2,1,0:T(8,128)(2,1)S(1)} %get-tuple-element.10.sa), custom_call_target="tpu_custom_call" | custom-call | flops 4294967296 | bytes 10485760 | tf_op jit(solution)/shard_map/panel_product/pallas_call | solution.py:432

commit v6 on v5

--- a/solution.py
+++ b/solution.py
@@ -225,11 +225,12 @@
         def tail(t, _):
             for d in range(2):
                 b_copy(d, t - MB).wait_recv()
-                sb[d, t] = rb[d, t - MB]
 
                 @pl.when(t < TB_R)
                 def _():
-                    b_copy(d, t).start()
+                    remote(rb.at[d, t - MB], rb.at[d, t], b_send.at[d], b_recv.at[d, t], z_to[d]).start()
+
+                sb[d, t] = rb[d, t - MB]
 
             for d in range(2):
                 b_share(d, t).start()
@@ -314,11 +315,12 @@
         def tail(t, _):
             for d in range(2):
                 a_copy(d, t - MA).wait_recv()
-                sa[d, t] = ra[d, t - MA]
 
                 @pl.when(t < TA_R)
                 def _():
-                    a_copy(d, t).start()
+                    remote(ra.at[d, t - MA], ra.at[d, t], a_send.at[d], a_recv.at[d, t], x_to[d]).start()
+
+                sa[d, t] = ra[d, t - MA]
 
             for d in range(2):
                 a_share(d, t).start()

time: 61.7 us -> 61.5 us (level)
  no operation moved by 1% of the time
where the time goes in v6:
time: 61.5 us; the launch traced here: 61.4 us
  Pallas kernels  61.4 us (100%)
    pallas_call x1, Pallas kernels, per_device(): pl.pallas_call(comm_kernel, out_shape=[jax.ShapeDtypeStruct((2, SB_R, 2,...  52.7 us
    pallas_call x1, Pallas kernels, per_device(): pl.pallas_call(product_kernel, out_shape=jax.ShapeDtypeStruct((n, LC * BS...  8.7 us

profile of v6, /device:TPU:1, one launch (start us, length us, event | category | flops | bytes accessed | tf_op | source)
XLA Modules:
  0.0 61.4 jit_solution(7706384729828995346)
XLA Ops:
  0.0 52.7 %spread_tiles.1 = (bf16[2,97,2,4,16,128]{5,4,3,2,1,0:T(8,128)(2,1)S(1)}, bf16[2,59,4,32,128]{4,3,2,1,0:T(8,128)(2,1)S(1)}, s32[2,8,128]{2,1,0:T(8,128)S(1)}) custom-call(s32[4]{0:T(128)} %panels_hbm.1, s32[1,16]{1,0:T(1,128)} %pos_hbm.1, bf16[16,128,128]{2,1,0:T(8,128)(2,1)} %x_hbm.1), custom_call_target="tpu_custom_call" | custom-call | tf_op jit(solution)/shard_map/spread_tiles/pallas_call | solution.py:399
  52.7 8.7 %panel_product.1 = f32[1024,1024]{1,0:T(8,128)} custom-call(s32[2,8,128]{2,1,0:T(8,128)S(1)} %get-tuple-element.8.meta, bf16[2,97,2,4,16,128]{5,4,3,2,1,0:T(8,128)(2,1)S(1)} %get-tuple-element.9.sb, bf16[2,59,4,32,128]{4,3,2,1,0:T(8,128)(2,1)S(1)} %get-tuple-element.10.sa), custom_call_target="tpu_custom_call" | custom-call | flops 4294967296 | bytes 10485760 | tf_op jit(solution)/shard_map/panel_product/pallas_call | solution.py:434
